TPU v7x, 256 devices: a whole 4x4x8 slice. The times are simulated.
256 devices in a mesh: gy: 64 (over x, y, z_hi, core), gz: 4 (over z_lo).
Axes of the slice: x: 4, y: 4, z: 8 (z_hi: 2, z_lo: 4; z = z_hi * 4 + z_lo), core: 2. Of those that a mesh axis runs over, the one named last changes fastest.
Arguments:
- efield_check: bfloat16 [3, 2048, 8, 1024], P(None, 'gy', None, 'gz'), may hold values from -6 to 6
- hfield_check: bfloat16 [3, 2048, 8, 1024], P(None, 'gy', None, 'gz'), may hold values from -6 to 6
- polar_check: bfloat16 [3, 2048, 8, 1024], P(None, 'gy', None, 'gz'), may hold values from -4 to 4
- rate_check: bfloat16 [3, 2048, 8, 1024], P(None, 'gy', None, 'gz'), may hold values from -4 to 4
- levels_check: bfloat16 [2, 2048, 8, 1024], P(None, 'gy', None, 'gz'), may hold values from 0.049804688 to 0.5
- efield_seed: float32 [3, 2048, 8, 1024], P(None, 'gy', None, 'gz'), may hold values from -6 to 6
- hfield_seed: float32 [3, 2048, 8, 1024], P(None, 'gy', None, 'gz'), may hold values from -6 to 6
- polar_seed: float32 [3, 2048, 8, 1024], P(None, 'gy', None, 'gz'), may hold values from -6 to 6
- rate_seed: float32 [3, 2048, 8, 1024], P(None, 'gy', None, 'gz'), may hold values from -6 to 6
- levels_seed: float32 [2, 2048, 8, 1024], P(None, 'gy', None, 'gz'), may hold values from -6 to 6
- material_labels: int32 [2048, 8, 1024], P('gy', None, 'gz'), may hold values from 0 to 3
- gain_labels: int32 [2048, 8, 1024], P('gy', None, 'gz'), may hold values 0 or 1
- inverse_table: float32 [4], replicated, may hold values from 0.08 to 1
- source_field: float32 [2048, 8, 1024], P('gy', None, 'gz'), may hold values from -6 to 6
- start_step: int32 [1], replicated, may hold values from 0 to 255
Outputs:
- efield_grad: float32 [3, 2048, 8, 1024], P(None, 'gy', None, 'gz')
- hfield_grad: float32 [3, 2048, 8, 1024], P(None, 'gy', None, 'gz')
- polar_grad: float32 [3, 2048, 8, 1024], P(None, 'gy', None, 'gz')
- rate_grad: float32 [3, 2048, 8, 1024], P(None, 'gy', None, 'gz')
- levels_grad: float32 [2, 2048, 8, 1024], P(None, 'gy', None, 'gz')
- cell_grad: float32 [2048, 8, 1024], P('gy', None, 'gz')
- table_grad: float32 [4], replicated
All inputs are finite; a program needn't handle non-finite values. No bound on the sum of `gain_labels` on one device may be relied on, other than what follows from the above.
Results may differ from a plain program's by a relative error of at most 0.0003.
Values may be sent and summed in bfloat16 or wider, within the bound.
No kernel may reach another device: no remote copies, remote signals or barrier semaphores. Data moves between devices by JAX's collectives and lax.ppermute only.
A program may use at most 64 MiB of HBM per device.

v0:
```python
import math
import jax
import jax.numpy as jnp
from jax import lax
from jax.sharding import PartitionSpec as P

MAGNETIC_STEP = 0.5
ELECTRIC_STEP = 0.5
TIME_STEP = 0.5
DAMPING = 0.9
STIFFNESS = 0.3
COUPLING = 0.4
PUMPING = 0.05
UPPER_DECAY = 0.02
LOWER_DECAY = 0.3
STIMULATED = 0.2
SOURCE_OMEGA = 0.35


def shifted(block, axis, distance):
    devices = range(lax.axis_size(axis))
    route = [(i - distance, i) for i in devices if i - distance in devices]
    return lax.ppermute(block, axis, route)


def front(values, axis):
    rest = lax.slice_in_dim(values, 1, values.shape[axis], axis=axis)
    border = jnp.zeros_like(lax.slice_in_dim(values, 0, 1, axis=axis))
    return jnp.concatenate([rest, border], axis)


def behind(values, axis):
    rest = lax.slice_in_dim(values, 0, values.shape[axis] - 1, axis=axis)
    border = jnp.zeros_like(lax.slice_in_dim(values, 0, 1, axis=axis))
    return jnp.concatenate([border, rest], axis)


def curl_from(along_x, along_y, along_z):
    return jnp.stack([along_y[2] - along_z[1], along_z[0] - along_x[2], along_x[1] - along_y[0]])


def curl_forward(field):
    front_row = shifted(field[:, :1], "gy", -1)
    front_column = shifted(field[:, :, :, :1], "gz", -1)
    along_y = jnp.concatenate([field[:, 1:], front_row], 1) - field
    along_z = jnp.concatenate([field[:, :, :, 1:], front_column], 3) - field
    along_x = front(field, 2) - field
    return curl_from(along_x, along_y, along_z)


def curl_backward(field):
    back_row = shifted(field[:, -1:], "gy", 1)
    back_column = shifted(field[:, :, :, -1:], "gz", 1)
    along_y = field - jnp.concatenate([back_row, field[:, :-1]], 1)
    along_z = field - jnp.concatenate([back_column, field[:, :, :, :-1]], 3)
    along_x = field - behind(field, 2)
    return curl_from(along_x, along_y, along_z)


def local_update(
    efield, polar_field, polar_rate, levels, curl_field, inverse, gain_region, source_push
):
    rate_next = (
        DAMPING * polar_rate
        - STIFFNESS * polar_field
        + COUPLING * gain_region * (levels[0] - levels[1]) * efield
    )
    polar_next = polar_field + TIME_STEP * rate_next
    forcing = ELECTRIC_STEP * curl_field - (polar_next - polar_field)
    forcing = jnp.concatenate([forcing[:2], forcing[2:] - source_push[None]], 0)
    efield_next = efield + inverse * forcing
    stimulated = STIMULATED * gain_region * jnp.sum(efield_next * rate_next, axis=0)
    upper = (
        levels[0]
        + TIME_STEP * (PUMPING * (1.0 - levels[0] - levels[1]) - UPPER_DECAY * levels[0])
        - stimulated
    )
    lower = levels[1] + TIME_STEP * (UPPER_DECAY * levels[0] - LOWER_DECAY * levels[1]) + stimulated
    return (efield_next, polar_next, rate_next, jnp.stack([upper, lower]))


def reverse_local(
    efield, polar_field, polar_rate, levels, curl_field, inverse, gain_region, source_push, seeds
):

    def update(first, second, third, fourth, fifth, sixth):
        return local_update(first, second, third, fourth, fifth, sixth, gain_region, source_push)

    unused, pullback = jax.vjp(update, efield, polar_field, polar_rate, levels, curl_field, inverse)
    return pullback(seeds)


def material_map(material_labels, inverse_table):
    inverse = jnp.zeros(material_labels.shape, jnp.float32)
    for label in range(inverse_table.shape[0]):
        inverse = inverse + jnp.where(
            material_labels == label, inverse_table[label], jnp.float32(0.0)
        )
    return inverse


def label_sums(material_labels, values, count):
    return jnp.stack(
        [
            jnp.sum(jnp.where(material_labels == label, values, jnp.float32(0.0)))
            for label in range(count)
        ]
    )


def step_total(material_labels, values, count):
    return lax.psum(label_sums(material_labels, values, count), ("gy", "gz"))


def on_device(
    efield_check,
    hfield_check,
    polar_check,
    rate_check,
    levels_check,
    efield_seed,
    hfield_seed,
    polar_seed,
    rate_seed,
    levels_seed,
    material_labels,
    gain_labels,
    inverse_table,
    source_field,
    start_step,
):
    count = inverse_table.shape[0]
    inverse = material_map(material_labels, inverse_table)
    gain_region = gain_labels.astype(jnp.float32)
    start = start_step[0].astype(jnp.float32)
    first_sine = jnp.sin(SOURCE_OMEGA * start)
    push_first = first_sine * source_field
    push_second = jnp.sin(SOURCE_OMEGA * (start + 1.0)) * source_field
    efield = efield_check.astype(jnp.float32)
    polar_field = polar_check.astype(jnp.float32)
    polar_rate = rate_check.astype(jnp.float32)
    levels = levels_check.astype(jnp.float32)
    hfield = hfield_check.astype(jnp.float32)
    hfield_mid = hfield - MAGNETIC_STEP * curl_forward(efield)
    curl_first = curl_backward(hfield_mid)
    state_one = local_update(
        efield, polar_field, polar_rate, levels, curl_first, inverse, gain_region, push_first
    )
    hfield_next = hfield_mid - MAGNETIC_STEP * curl_forward(state_one[0])
    curl_second = curl_backward(hfield_next)
    back_e, back_p, back_q, back_n, back_c, grad_second = reverse_local(
        state_one[0],
        state_one[1],
        state_one[2],
        state_one[3],
        curl_second,
        inverse,
        gain_region,
        push_second,
        (efield_seed, polar_seed, rate_seed, levels_seed),
    )
    h_back = hfield_seed + curl_forward(back_c)
    e_back = back_e - MAGNETIC_STEP * curl_backward(h_back)
    last_e, polar_grad, rate_grad, levels_grad, last_c, grad_first = reverse_local(
        efield,
        polar_field,
        polar_rate,
        levels,
        curl_first,
        inverse,
        gain_region,
        push_first,
        (e_back, back_p, back_q, back_n),
    )
    hfield_grad = h_back + curl_forward(last_c)
    efield_grad = last_e - MAGNETIC_STEP * curl_backward(hfield_grad)
    cell_grad = grad_second + grad_first
    cells = (
        material_labels.shape[0]
        * material_labels.shape[1]
        * material_labels.shape[2]
        * lax.axis_size("gy")
        * lax.axis_size("gz")
    )
    totals = step_total(material_labels, grad_second, count) + step_total(
        material_labels, grad_first, count
    )
    table_grad = totals * (1.0 / math.sqrt(cells))
    return (efield_grad, hfield_grad, polar_grad, rate_grad, levels_grad, cell_grad, table_grad)


def solution(mesh):
    placed = (
        P(None, "gy", None, "gz"),
        P(None, "gy", None, "gz"),
        P(None, "gy", None, "gz"),
        P(None, "gy", None, "gz"),
        P(None, "gy", None, "gz"),
        P(None, "gy", None, "gz"),
        P(None, "gy", None, "gz"),
        P(None, "gy", None, "gz"),
        P(None, "gy", None, "gz"),
        P(None, "gy", None, "gz"),
        P("gy", None, "gz"),
        P("gy", None, "gz"),
        P(),
        P("gy", None, "gz"),
        P(),
    )
    return jax.shard_map(
        on_device,
        mesh=mesh,
        in_specs=placed,
        out_specs=(
            P(None, "gy", None, "gz"),
            P(None, "gy", None, "gz"),
            P(None, "gy", None, "gz"),
            P(None, "gy", None, "gz"),
            P(None, "gy", None, "gz"),
            P("gy", None, "gz"),
            P(),
        ),
        check_vma=False,
    )
```

profile of v0, /device:TPU:2, one launch (start us, length us, event | category | flops | bytes accessed | tf_op | source)
XLA Modules:
  0.0 215.5 jit_solution(16821565105719444470)
XLA Ops:
  1.7 1.3 collective-permute-start.1
  3.0 11.0 %collective-permute-start = (f32[3,1,8,256]{3,2,1,0:T(8,128)S(1)}, f32[3,1,8,256]{3,2,1,0:T(8,128)S(1)}, u32[]{:S(2)}, u32[]{:S(2)}) collective-permute-start(f32[3,1,8,256]{3,2,1,0:T(8,128)S(1)} %slice.410), channel_id=1, source_target_pairs={{4,0},{8,4},{12,8},{16,12},{20,16},{24,20},{28,24},{32,28},{36,32}... | collective-permute-start | bytes 73736 | tf_op jit(solution)/shard_map/ppermute | solution.py:23
  17.4 4.3 %collective-permute-start.3 = (f32[3,32,8,1]{3,2,1,0:T(8,128)S(1)}, f32[3,32,8,1]{3,2,1,0:T(8,128)S(1)}, u32[]{:S(2)}, u32[]{:S(2)}) collective-permute-start(f32[3,32,8,1]{3,2,1,0:T(8,128)S(1)} %slice.423), channel_id=1, source_target_pairs={{0,1},{1,2},{2,3},{4,5},{5,6},{6,7},{8,9},{9,10},{10,11},{12,13},{... | collective-permute-start | bytes 9224 | tf_op jit(solution)/shard_map/ppermute | solution.py:23
  21.7 5.1 %collective-permute-start.2 = (f32[3,1,8,256]{3,2,1,0:T(8,128)S(1)}, f32[3,1,8,256]{3,2,1,0:T(8,128)S(1)}, u32[]{:S(2)}, u32[]{:S(2)}) collective-permute-start(f32[3,1,8,256]{3,2,1,0:T(8,128)S(1)} %slice.420), channel_id=1, source_target_pairs={{0,4},{4,8},{8,12},{12,16},{16,20},{20,24},{24,28},{28,32},{32,36}... | collective-permute-start | bytes 73736 | tf_op jit(solution)/shard_map/ppermute | solution.py:23
  26.8 2.8 %select_add_fusion.2 = (f32[32,8,256]{2,1,0:T(8,128)S(1)}, pred[32,8,256]{2,1,0:T(8,128)(4,1)S(1)}, pred[32,8,256]{2,1,0:T(8,128)(4,1)S(1)}, pred[32,8,256]{2,1,...) fusion(f32[]{:T(128)} %bitcast.6, f32[]{:T(128)} %bitcast.5, f32[]{:T(128)} %bitcast.4, ...), kind=kLoop, calls=%fused_computation.118 | loop fusion | flops 983040 | bytes 1835024 | tf_op jit(solution)/shard_map/add | solution.py:96
  30.5 8.8 %collective-permute-done.2 = f32[3,1,8,256]{3,2,1,0:T(8,128)S(1)} collective-permute-done((f32[3,1,8,256]{3,2,1,0:T(8,128)S(1)}, f32[3,1,8,256]{3,2,1,0:T(8,128)S(1)}, u32[]{:S(2)}, u32[]{:S(2)}) %collective-permute-start.2) | collective-permute-done | bytes 24608 | tf_op jit(solution)/shard_map/ppermute | solution.py:23
  42.5 1.4 collective-permute-start.5
  43.9 1.9 collective-permute-start.4
  46.5 5.8 %collective-permute-done.5 = f32[3,32,8,1]{3,2,1,0:T(8,128)S(1)} collective-permute-done((f32[3,32,8,1]{3,2,1,0:T(8,128)S(1)}, f32[3,32,8,1]{3,2,1,0:T(8,128)S(1)}, u32[]{:S(2)}, u32[]{:S(2)}) %collective-permute-start.5) | collective-permute-done | bytes 3104 | tf_op jit(solution)/shard_map/ppermute | solution.py:23
  53.0 2.0 collective-permute-start.7
  55.0 1.9 collective-permute-start.6
  57.2 5.5 %collective-permute-done.7 = f32[3,32,8,1]{3,2,1,0:T(8,128)S(1)} collective-permute-done((f32[3,32,8,1]{3,2,1,0:T(8,128)S(1)}, f32[3,32,8,1]{3,2,1,0:T(8,128)S(1)}, u32[]{:S(2)}, u32[]{:S(2)}) %collective-permute-start.7) | collective-permute-done | bytes 3104 | tf_op jit(solution)/shard_map/ppermute | solution.py:23
  62.8 7.7 %collective-permute-done.6 = f32[3,1,8,256]{3,2,1,0:T(8,128)S(1)} collective-permute-done((f32[3,1,8,256]{3,2,1,0:T(8,128)S(1)}, f32[3,1,8,256]{3,2,1,0:T(8,128)S(1)}, u32[]{:S(2)}, u32[]{:S(2)}) %collective-permute-start.6) | collective-permute-done | bytes 24608 | tf_op jit(solution)/shard_map/ppermute | solution.py:23
  75.1 1.3 collective-permute-start.9
  76.4 1.9 collective-permute-start.8
  79.8 5.0 %collective-permute-done.9 = f32[3,32,8,1]{3,2,1,0:T(8,128)S(1)} collective-permute-done((f32[3,32,8,1]{3,2,1,0:T(8,128)S(1)}, f32[3,32,8,1]{3,2,1,0:T(8,128)S(1)}, u32[]{:S(2)}, u32[]{:S(2)}) %collective-permute-start.9) | collective-permute-done | bytes 3104 | tf_op jit(solution)/shard_map/ppermute | solution.py:23
  85.3 1.1 copy-done.2
  86.7 2.0 collective-permute-start.11
  88.8 1.9 collective-permute-start.10
  90.8 4.8 %collective-permute-done.11 = f32[3,32,8,1]{3,2,1,0:T(8,128)S(1)} collective-permute-done((f32[3,32,8,1]{3,2,1,0:T(8,128)S(1)}, f32[3,32,8,1]{3,2,1,0:T(8,128)S(1)}, u32[]{:S(2)}, u32[]{:S(2)}) %collective-permute-start.11) | collective-permute-done | bytes 3104 | tf_op jit(solution)/shard_map/ppermute | solution.py:23
  95.6 7.6 %collective-permute-done.10 = f32[3,1,8,256]{3,2,1,0:T(8,128)S(1)} collective-permute-done((f32[3,1,8,256]{3,2,1,0:T(8,128)S(1)}, f32[3,1,8,256]{3,2,1,0:T(8,128)S(1)}, u32[]{:S(2)}, u32[]{:S(2)}) %collective-permute-start.10) | collective-permute-done | bytes 24608 | tf_op jit(solution)/shard_map/ppermute | solution.py:23
  104.9 1.6 multiply_add_fusion
  107.4 1.3 collective-permute-start.13
  108.7 2.1 collective-permute-start.12
  110.8 1.6 select_reduce_fusion.7
  112.4 5.1 %maximum_add_fusion.2 = f32[4]{0:T(128)S(1)} fusion(f32[1]{0:T(128)} %bitcast.19, f32[1]{0:T(128)} %bitcast.18, f32[1]{0:T(128)} %bitcast.17, f32[1]{0:T(128)} %bitcast.16, f32[1]{0:T(128)} %bitcast.23, f32[1]{0:T(128)} %bitcast.22, f32[1]{0:T(128)} %bitcast.21, f32[1]{0:T(128)} %bitcast.20), kind=kLoop, calls=%fused_computation.132 | loop fusion | flops 28 | bytes 48 | tf_op jit(solution)/shard_map/add | solution.py:185
  118.7 76.3 %psum.16 = f32[4]{0:T(128)S(1)} all-reduce(f32[4]{0:T(128)S(1)} %maximum_add_fusion.2), channel_id=1, replica_groups=mesh['gy'=64,'gz'=4] {'gy','gz'}, use_global_device_ids=true, to_apply=%region_9.10 | all-reduce | flops 4 | bytes 32 | tf_op jit(solution)/shard_map/psum | solution.py:112
  195.4 1.3 maximum_subtract_fusion.11
  198.1 2.1 collective-permute-start.15
  200.2 1.9 collective-permute-start.14
  202.7 6.1 %collective-permute-done.15 = f32[3,32,8,1]{3,2,1,0:T(8,128)S(1)} collective-permute-done((f32[3,32,8,1]{3,2,1,0:T(8,128)S(1)}, f32[3,32,8,1]{3,2,1,0:T(8,128)S(1)}, u32[]{:S(2)}, u32[]{:S(2)}) %collective-permute-start.15) | collective-permute-done | bytes 3104 | tf_op jit(solution)/shard_map/ppermute | solution.py:23
  208.8 5.1 %collective-permute-done.14 = f32[3,1,8,256]{3,2,1,0:T(8,128)S(1)} collective-permute-done((f32[3,1,8,256]{3,2,1,0:T(8,128)S(1)}, f32[3,1,8,256]{3,2,1,0:T(8,128)S(1)}, u32[]{:S(2)}, u32[]{:S(2)}) %collective-permute-start.14) | collective-permute-done | bytes 24608 | tf_op jit(solution)/shard_map/ppermute | solution.py:23
  (130 shorter events, 23.5 us)
Async XLA Ops:
  0.6 2.3 %copy-start = (bf16[3,32,8,256]{3,2,1,0:T(8,128)(2,1)S(1)}, bf16[3,32,8,256]{3,2,1,0:T(8,128)(2,1)}, u32[]{:S(2)}) copy-start(bf16[3,32,8,256]{3,2,1,0:T(8,128)(2,1)} %param.15) | copy-start | bytes 1179652
  1.7 14.2 %collective-permute-start.1 = (f32[3,32,8,1]{3,2,1,0:T(8,128)S(1)}, f32[3,32,8,1]{3,2,1,0:T(8,128)S(1)}, u32[]{:S(2)}, u32[]{:S(2)}) collective-permute-start(f32[3,32,8,1]{3,2,1,0:T(8,128)S(1)} %slice.413), channel_id=1, source_target_pairs={{1,0},{2,1},{3,2},{5,4},{6,5},{7,6},{9,8},{10,9},{11,10},{13,12},{... | collective-permute-start | bytes 9224 | tf_op jit(solution)/shard_map/ppermute | solution.py:23
  3.0 11.0 %copy-start.20 = (f32[4]{0:T(128)S(1)}, f32[4]{0:T(128)}, u32[]{:S(2)}) copy-start(f32[4]{0:T(128)} %param.27) | copy-start | bytes 52
  3.0 12.8 %collective-permute-start = (f32[3,1,8,256]{3,2,1,0:T(8,128)S(1)}, f32[3,1,8,256]{3,2,1,0:T(8,128)S(1)}, u32[]{:S(2)}, u32[]{:S(2)}) collective-permute-start(f32[3,1,8,256]{3,2,1,0:T(8,128)S(1)} %slice.410), channel_id=1, source_target_pairs={{4,0},{8,4},{12,8},{16,12},{20,16},{24,20},{28,24},{32,28},{36,32}... | collective-permute-start | bytes 73736 | tf_op jit(solution)/shard_map/ppermute | solution.py:23
  17.2 9.6 %copy-start.13 = (s32[32,8,256]{2,1,0:T(8,128)S(1)}, s32[32,8,256]{2,1,0:T(8,128)}, u32[]{:S(2)}) copy-start(s32[32,8,256]{2,1,0:T(8,128)} %param.26) | copy-start | bytes 786436
  17.2 9.6 %copy-start.19 = (s32[32,8,256]{2,1,0:T(8,128)S(1)}, s32[32,8,256]{2,1,0:T(8,128)}, u32[]{:S(2)}) copy-start(s32[32,8,256]{2,1,0:T(8,128)} %param.25) | copy-start | bytes 786436
  17.4 13.0 %collective-permute-start.3 = (f32[3,32,8,1]{3,2,1,0:T(8,128)S(1)}, f32[3,32,8,1]{3,2,1,0:T(8,128)S(1)}, u32[]{:S(2)}, u32[]{:S(2)}) collective-permute-start(f32[3,32,8,1]{3,2,1,0:T(8,128)S(1)} %slice.423), channel_id=1, source_target_pairs={{0,1},{1,2},{2,3},{4,5},{5,6},{6,7},{8,9},{9,10},{10,11},{12,13},{... | collective-permute-start | bytes 9224 | tf_op jit(solution)/shard_map/ppermute | solution.py:23
  21.7 17.5 %collective-permute-start.2 = (f32[3,1,8,256]{3,2,1,0:T(8,128)S(1)}, f32[3,1,8,256]{3,2,1,0:T(8,128)S(1)}, u32[]{:S(2)}, u32[]{:S(2)}) collective-permute-start(f32[3,1,8,256]{3,2,1,0:T(8,128)S(1)} %slice.420), channel_id=1, source_target_pairs={{0,4},{4,8},{8,12},{12,16},{16,20},{20,24},{24,28},{28,32},{32,36}... | collective-permute-start | bytes 73736 | tf_op jit(solution)/shard_map/ppermute | solution.py:23
  39.6 1.1 copy-start.4
  42.4 3.4 %copy-start.5 = (f32[2,32,8,256]{3,2,1,0:T(8,128)S(1)}, f32[2,32,8,256]{3,2,1,0:T(8,128)}, u32[]{:S(2)}) copy-start(f32[2,32,8,256]{3,2,1,0:T(8,128)} %param.24) | copy-start | bytes 1572868
  42.5 9.8 %collective-permute-start.5 = (f32[3,32,8,1]{3,2,1,0:T(8,128)S(1)}, f32[3,32,8,1]{3,2,1,0:T(8,128)S(1)}, u32[]{:S(2)}, u32[]{:S(2)}) collective-permute-start(f32[3,32,8,1]{3,2,1,0:T(8,128)S(1)} %slice.437), channel_id=1, source_target_pairs={{1,0},{2,1},{3,2},{5,4},{6,5},{7,6},{9,8},{10,9},{11,10},{13,12},{... | collective-permute-start | bytes 9224 | tf_op jit(solution)/shard_map/ppermute | solution.py:23
  43.9 8.4 %collective-permute-start.4 = (f32[3,1,8,256]{3,2,1,0:T(8,128)S(1)}, f32[3,1,8,256]{3,2,1,0:T(8,128)S(1)}, u32[]{:S(2)}, u32[]{:S(2)}) collective-permute-start(f32[3,1,8,256]{3,2,1,0:T(8,128)S(1)} %slice.434), channel_id=1, source_target_pairs={{4,0},{8,4},{12,8},{16,12},{20,16},{24,20},{28,24},{32,28},{36,32}... | collective-permute-start | bytes 73736 | tf_op jit(solution)/shard_map/ppermute | solution.py:23
  53.0 9.7 %collective-permute-start.7 = (f32[3,32,8,1]{3,2,1,0:T(8,128)S(1)}, f32[3,32,8,1]{3,2,1,0:T(8,128)S(1)}, u32[]{:S(2)}, u32[]{:S(2)}) collective-permute-start(f32[3,32,8,1]{3,2,1,0:T(8,128)S(1)} %slice.447), channel_id=1, source_target_pairs={{0,1},{1,2},{2,3},{4,5},{5,6},{6,7},{8,9},{9,10},{10,11},{12,13},{... | collective-permute-start | bytes 9224 | tf_op jit(solution)/shard_map/ppermute | solution.py:23
  55.0 15.4 %collective-permute-start.6 = (f32[3,1,8,256]{3,2,1,0:T(8,128)S(1)}, f32[3,1,8,256]{3,2,1,0:T(8,128)S(1)}, u32[]{:S(2)}, u32[]{:S(2)}) collective-permute-start(f32[3,1,8,256]{3,2,1,0:T(8,128)S(1)} %slice.444), channel_id=1, source_target_pairs={{0,4},{4,8},{8,12},{12,16},{16,20},{20,24},{24,28},{28,32},{32,36}... | collective-permute-start | bytes 73736 | tf_op jit(solution)/shard_map/ppermute | solution.py:23
  71.6 1.1 copy-start.16
  73.2 1.1 copy-start.6
  73.2 1.4 copy-start.17
  73.3 1.3 copy-start.21
  75.1 9.7 %collective-permute-start.9 = (f32[3,32,8,1]{3,2,1,0:T(8,128)S(1)}, f32[3,32,8,1]{3,2,1,0:T(8,128)S(1)}, u32[]{:S(2)}, u32[]{:S(2)}) collective-permute-start(f32[3,32,8,1]{3,2,1,0:T(8,128)S(1)} %slice.461), channel_id=1, source_target_pairs={{1,0},{2,1},{3,2},{5,4},{6,5},{7,6},{9,8},{10,9},{11,10},{13,12},{... | collective-permute-start | bytes 9224 | tf_op jit(solution)/shard_map/ppermute | solution.py:23
  76.4 8.4 %collective-permute-start.8 = (f32[3,1,8,256]{3,2,1,0:T(8,128)S(1)}, f32[3,1,8,256]{3,2,1,0:T(8,128)S(1)}, u32[]{:S(2)}, u32[]{:S(2)}) collective-permute-start(f32[3,1,8,256]{3,2,1,0:T(8,128)S(1)} %slice.458), channel_id=1, source_target_pairs={{4,0},{8,4},{12,8},{16,12},{20,16},{24,20},{28,24},{32,28},{36,32}... | collective-permute-start | bytes 73736 | tf_op jit(solution)/shard_map/ppermute | solution.py:23
  85.1 1.3 copy-start.2
  85.3 17.9 %copy-start.7 = (f32[1,32,8,256]{3,2,1,0:T(8,128)}, f32[1,32,8,256]{3,2,1,0:T(8,128)S(1)}, u32[]{:S(2)}) copy-start(f32[1,32,8,256]{3,2,1,0:T(8,128)S(1)} %get-tuple-element.59) | copy-start | bytes 786436
  85.3 17.9 %copy-start.9 = (f32[1,32,8,256]{3,2,1,0:T(8,128)}, f32[1,32,8,256]{3,2,1,0:T(8,128)S(1)}, u32[]{:S(2)}) copy-start(f32[1,32,8,256]{3,2,1,0:T(8,128)S(1)} %get-tuple-element.60) | copy-start | bytes 786436
  85.3 17.9 %copy-start.11 = (f32[1,32,8,256]{3,2,1,0:T(8,128)}, f32[1,32,8,256]{3,2,1,0:T(8,128)S(1)}, u32[]{:S(2)}) copy-start(f32[1,32,8,256]{3,2,1,0:T(8,128)S(1)} %get-tuple-element.61) | copy-start | bytes 786436
  86.7 8.9 %collective-permute-start.11 = (f32[3,32,8,1]{3,2,1,0:T(8,128)S(1)}, f32[3,32,8,1]{3,2,1,0:T(8,128)S(1)}, u32[]{:S(2)}, u32[]{:S(2)}) collective-permute-start(f32[3,32,8,1]{3,2,1,0:T(8,128)S(1)} %slice.471), channel_id=1, source_target_pairs={{0,1},{1,2},{2,3},{4,5},{5,6},{6,7},{8,9},{9,10},{10,11},{12,13},{... | collective-permute-start | bytes 9224 | tf_op jit(solution)/shard_map/ppermute | solution.py:23
  88.8 14.5 %collective-permute-start.10 = (f32[3,1,8,256]{3,2,1,0:T(8,128)S(1)}, f32[3,1,8,256]{3,2,1,0:T(8,128)S(1)}, u32[]{:S(2)}, u32[]{:S(2)}) collective-permute-start(f32[3,1,8,256]{3,2,1,0:T(8,128)S(1)} %slice.468), channel_id=1, source_target_pairs={{0,4},{4,8},{8,12},{12,16},{16,20},{20,24},{24,28},{28,32},{32,36}... | collective-permute-start | bytes 73736 | tf_op jit(solution)/shard_map/ppermute | solution.py:23
  107.4 88.0 %collective-permute-start.13 = (f32[3,32,8,1]{3,2,1,0:T(8,128)}, f32[3,32,8,1]{3,2,1,0:T(8,128)}, u32[]{:S(2)}, u32[]{:S(2)}) collective-permute-start(f32[3,32,8,1]{3,2,1,0:T(8,128)} %slice.483), channel_id=1, source_target_pairs={{1,0},{2,1},{3,2},{5,4},{6,5},{7,6},{9,8},{10,9},{11,10},{13,12},{... | collective-permute-start | bytes 9224 | tf_op jit(solution)/shard_map/ppermute | solution.py:23
  108.7 86.7 %collective-permute-start.12 = (f32[3,1,8,256]{3,2,1,0:T(8,128)S(1)}, f32[3,1,8,256]{3,2,1,0:T(8,128)S(1)}, u32[]{:S(2)}, u32[]{:S(2)}) collective-permute-start(f32[3,1,8,256]{3,2,1,0:T(8,128)S(1)} %slice.480), channel_id=1, source_target_pairs={{4,0},{8,4},{12,8},{16,12},{20,16},{24,20},{28,24},{32,28},{36,32}... | collective-permute-start | bytes 73736 | tf_op jit(solution)/shard_map/ppermute | solution.py:23
  196.7 1.1 copy-start.12
  198.0 15.9 %copy-start.1 = (f32[3,32,8,256]{3,2,1,0:T(8,128)}, f32[3,32,8,256]{3,2,1,0:T(8,128)S(1)}, u32[]{:S(2)}) copy-start(f32[3,32,8,256]{3,2,1,0:T(8,128)S(1)} %maximum_add_fusion.1) | copy-start | bytes 2359300
  198.1 10.7 %collective-permute-start.15 = (f32[3,32,8,1]{3,2,1,0:T(8,128)S(1)}, f32[3,32,8,1]{3,2,1,0:T(8,128)S(1)}, u32[]{:S(2)}, u32[]{:S(2)}) collective-permute-start(f32[3,32,8,1]{3,2,1,0:T(8,128)S(1)} %slice.493), channel_id=1, source_target_pairs={{0,1},{1,2},{2,3},{4,5},{5,6},{6,7},{8,9},{9,10},{10,11},{12,13},{... | collective-permute-start | bytes 9224 | tf_op jit(solution)/shard_map/ppermute | solution.py:23
  200.2 13.7 %collective-permute-start.14 = (f32[3,1,8,256]{3,2,1,0:T(8,128)S(1)}, f32[3,1,8,256]{3,2,1,0:T(8,128)S(1)}, u32[]{:S(2)}, u32[]{:S(2)}) collective-permute-start(f32[3,1,8,256]{3,2,1,0:T(8,128)S(1)} %slice.490), channel_id=1, source_target_pairs={{0,4},{4,8},{8,12},{12,16},{16,20},{20,24},{24,28},{28,32},{32,36}... | collective-permute-start | bytes 73736 | tf_op jit(solution)/shard_map/ppermute | solution.py:23
  (7 other events, 6.5 us)
where the time goes:
time: 217 us; the launch traced here: 216 us
  blocking collectives  76.3 us (35%)
  waiting for transfers between devices  56.5 us (26%)
  starting transfers between devices  43.4 us (20%)
  other arithmetic  23.4 us (11%)
  local copies, waits for them, and re-layouts  13.7 us (6%)
  between operations  2.27 us (1%)
    psum x1, blocking collectives, step_total(): return lax.psum(label_sums(material_labels, values, count), ('gy', 'gz'))  76.3 us
    ppermute x16, waiting for transfers between devices, shifted(): return lax.ppermute(block, axis, route)  56.5 us
    ppermute x16, starting transfers between devices, shifted(): return lax.ppermute(block, axis, route)  43.4 us
    unnamed x46, local copies, waits for them, and re-layouts  8.78 us
    add x1, other arithmetic, on_device(): step_total(material_labels, grad_second, count)  5.11 us
  transfers between devices with their start and end apart: 16, of which 9 were waited for; matrix products, arithmetic and copies ran while one was open for 7% of the time, Pallas kernels for 0%

commit v1 on v0

--- a/solution.py
+++ b/solution.py
@@ -3,6 +3,7 @@
 import jax.numpy as jnp
 from jax import lax
 from jax.sharding import PartitionSpec as P
+from jax.lax import psum
 
 MAGNETIC_STEP = 0.5
 ELECTRIC_STEP = 0.5
@@ -17,6 +18,12 @@
 SOURCE_OMEGA = 0.35
 
 
+def detail_goods(content, dev_axis, net_axis):
+    last = psum(content, axis_name=dev_axis)
+    step_out = psum(last, axis_name=net_axis)
+    return step_out
+
+
 def shifted(block, axis, distance):
     devices = range(lax.axis_size(axis))
     route = [(i - distance, i) for i in devices if i - distance in devices]
@@ -109,7 +116,7 @@
 
 
 def step_total(material_labels, values, count):
-    return lax.psum(label_sums(material_labels, values, count), ("gy", "gz"))
+    return detail_goods(label_sums(material_labels, values, count), "gy", "gz")
 
 
 def on_device(

time: 217 us -> 345 us (1.59)
  the two profiles are of different devices: /device:TPU:2 before, /device:TPU:32 now
where the time goes in v1:
time: 345 us; the launch traced here: 344 us
  blocking collectives  213 us (62%)
  starting transfers between devices  44.3 us (13%)
  waiting for transfers between devices  41.7 us (12%)
  other arithmetic  27.6 us (8%)
  local copies, waits for them, and re-layouts  14.7 us (4%)
    psum x1, blocking collectives, detail_goods(): last = psum(content, axis_name=dev_axis)  203 us
    ppermute x16, starting transfers between devices, shifted(): return lax.ppermute(block, axis, route)  44.3 us
    ppermute x16, waiting for transfers between devices, shifted(): return lax.ppermute(block, axis, route)  41.7 us
    psum x1, blocking collectives, detail_goods(): step_out = psum(last, axis_name=net_axis)  10.2 us
    unnamed x68, local copies, waits for them, and re-layouts  9.8 us
  transfers between devices with their start and end apart: 16, of which 6 were waited for; matrix products, arithmetic and copies ran while one was open for 3% of the time, Pallas kernels for 0%

profile of v1, /device:TPU:32, one launch (start us, length us, event | category | flops | bytes accessed | tf_op | source)
XLA Modules:
  0.0 344.0 jit_solution(664427434805603892)
XLA Ops:
  1.7 3.7 %collective-permute-start.1 = (f32[3,32,8,1]{3,2,1,0:T(8,128)S(1)}, f32[3,32,8,1]{3,2,1,0:T(8,128)S(1)}, u32[]{:S(2)}, u32[]{:S(2)}) collective-permute-start(f32[3,32,8,1]{3,2,1,0:T(8,128)S(1)} %slice.413), channel_id=1, source_target_pairs={{1,0},{2,1},{3,2},{5,4},{6,5},{7,6},{9,8},{10,9},{11,10},{13,12},{... | collective-permute-start | bytes 9224 | tf_op jit(solution)/shard_map/ppermute | solution.py:30
  5.4 1.3 collective-permute-start
  8.6 6.0 %collective-permute-done.1 = f32[3,32,8,1]{3,2,1,0:T(8,128)S(1)} collective-permute-done((f32[3,32,8,1]{3,2,1,0:T(8,128)S(1)}, f32[3,32,8,1]{3,2,1,0:T(8,128)S(1)}, u32[]{:S(2)}, u32[]{:S(2)}) %collective-permute-start.1) | collective-permute-done | bytes 3104 | tf_op jit(solution)/shard_map/ppermute | solution.py:30
  16.2 3.6 %collective-permute-start.3 = (f32[3,32,8,1]{3,2,1,0:T(8,128)S(1)}, f32[3,32,8,1]{3,2,1,0:T(8,128)S(1)}, u32[]{:S(2)}, u32[]{:S(2)}) collective-permute-start(f32[3,32,8,1]{3,2,1,0:T(8,128)S(1)} %slice.423), channel_id=1, source_target_pairs={{0,1},{1,2},{2,3},{4,5},{5,6},{6,7},{8,9},{9,10},{10,11},{12,13},{... | collective-permute-start | bytes 9224 | tf_op jit(solution)/shard_map/ppermute | solution.py:30
  19.8 5.4 %collective-permute-start.2 = (f32[3,1,8,256]{3,2,1,0:T(8,128)S(1)}, f32[3,1,8,256]{3,2,1,0:T(8,128)S(1)}, u32[]{:S(2)}, u32[]{:S(2)}) collective-permute-start(f32[3,1,8,256]{3,2,1,0:T(8,128)S(1)} %slice.420), channel_id=1, source_target_pairs={{0,4},{4,8},{8,12},{12,16},{16,20},{20,24},{24,28},{28,32},{32,36}... | collective-permute-start | bytes 73736 | tf_op jit(solution)/shard_map/ppermute | solution.py:30
  25.2 2.8 select_add_fusion.2
  32.1 3.8 %collective-permute-start.5 = (f32[3,32,8,1]{3,2,1,0:T(8,128)S(1)}, f32[3,32,8,1]{3,2,1,0:T(8,128)S(1)}, u32[]{:S(2)}, u32[]{:S(2)}) collective-permute-start(f32[3,32,8,1]{3,2,1,0:T(8,128)S(1)} %slice.437), channel_id=1, source_target_pairs={{1,0},{2,1},{3,2},{5,4},{6,5},{7,6},{9,8},{10,9},{11,10},{13,12},{... | collective-permute-start | bytes 9224 | tf_op jit(solution)/shard_map/ppermute | solution.py:30
  35.9 1.3 collective-permute-start.4
  37.8 7.2 %collective-permute-done.5 = f32[3,32,8,1]{3,2,1,0:T(8,128)S(1)} collective-permute-done((f32[3,32,8,1]{3,2,1,0:T(8,128)S(1)}, f32[3,32,8,1]{3,2,1,0:T(8,128)S(1)}, u32[]{:S(2)}, u32[]{:S(2)}) %collective-permute-start.5) | collective-permute-done | bytes 3104 | tf_op jit(solution)/shard_map/ppermute | solution.py:30
  45.8 4.4 %collective-permute-start.7 = (f32[3,32,8,1]{3,2,1,0:T(8,128)S(1)}, f32[3,32,8,1]{3,2,1,0:T(8,128)S(1)}, u32[]{:S(2)}, u32[]{:S(2)}) collective-permute-start(f32[3,32,8,1]{3,2,1,0:T(8,128)S(1)} %slice.447), channel_id=1, source_target_pairs={{0,1},{1,2},{2,3},{4,5},{5,6},{6,7},{8,9},{9,10},{10,11},{12,13},{... | collective-permute-start | bytes 9224 | tf_op jit(solution)/shard_map/ppermute | solution.py:30
  50.2 3.0 collective-permute-start.6
  53.5 5.9 %collective-permute-done.7 = f32[3,32,8,1]{3,2,1,0:T(8,128)S(1)} collective-permute-done((f32[3,32,8,1]{3,2,1,0:T(8,128)S(1)}, f32[3,32,8,1]{3,2,1,0:T(8,128)S(1)}, u32[]{:S(2)}, u32[]{:S(2)}) %collective-permute-start.7) | collective-permute-done | bytes 3104 | tf_op jit(solution)/shard_map/ppermute | solution.py:30
  64.0 1.9 collective-permute-start.9
  65.9 1.3 collective-permute-start.8
  69.7 8.3 %collective-permute-done.9 = f32[3,32,8,1]{3,2,1,0:T(8,128)S(1)} collective-permute-done((f32[3,32,8,1]{3,2,1,0:T(8,128)S(1)}, f32[3,32,8,1]{3,2,1,0:T(8,128)S(1)}, u32[]{:S(2)}, u32[]{:S(2)}) %collective-permute-start.9) | collective-permute-done | bytes 3104 | tf_op jit(solution)/shard_map/ppermute | solution.py:30
  78.5 1.2 copy-done.2
  80.0 3.6 %collective-permute-start.11 = (f32[3,32,8,1]{3,2,1,0:T(8,128)S(1)}, f32[3,32,8,1]{3,2,1,0:T(8,128)S(1)}, u32[]{:S(2)}, u32[]{:S(2)}) collective-permute-start(f32[3,32,8,1]{3,2,1,0:T(8,128)S(1)} %slice.471), channel_id=1, source_target_pairs={{0,1},{1,2},{2,3},{4,5},{5,6},{6,7},{8,9},{9,10},{10,11},{12,13},{... | collective-permute-start | bytes 9224 | tf_op jit(solution)/shard_map/ppermute | solution.py:30
  83.6 3.0 collective-permute-start.10
  86.7 5.9 %collective-permute-done.11 = f32[3,32,8,1]{3,2,1,0:T(8,128)S(1)} collective-permute-done((f32[3,32,8,1]{3,2,1,0:T(8,128)S(1)}, f32[3,32,8,1]{3,2,1,0:T(8,128)S(1)}, u32[]{:S(2)}, u32[]{:S(2)}) %collective-permute-start.11) | collective-permute-done | bytes 3104 | tf_op jit(solution)/shard_map/ppermute | solution.py:30
  93.7 1.3 fusion.1
  95.0 1.6 multiply_add_fusion
  97.4 1.6 select_reduce_fusion.7
  99.0 5.1 %maximum_add_fusion.2 = f32[4]{0:T(128)S(1)} fusion(f32[1]{0:T(128)} %bitcast.19, f32[1]{0:T(128)} %bitcast.18, f32[1]{0:T(128)} %bitcast.17, f32[1]{0:T(128)} %bitcast.16, f32[1]{0:T(128)} %bitcast.23, f32[1]{0:T(128)} %bitcast.22, f32[1]{0:T(128)} %bitcast.21, f32[1]{0:T(128)} %bitcast.20), kind=kLoop, calls=%fused_computation.132 | loop fusion | flops 28 | bytes 48 | tf_op jit(solution)/shard_map/add | solution.py:192
  104.1 203.0 %psum.33 = f32[4]{0:T(128)S(1)} all-reduce(f32[4]{0:T(128)S(1)} %maximum_add_fusion.2), channel_id=1, replica_groups=mesh['gy'=64,'gz'=4] {'gy'}, use_global_device_ids=true, to_apply=%region_9.10 | all-reduce | flops 4 | bytes 32 | tf_op jit(solution)/shard_map/psum | solution.py:22
  308.3 1.9 collective-permute-start.13
  310.2 1.3 collective-permute-start.12
  311.6 2.8 pad_add_fusion
  314.4 10.2 %psum.32 = f32[4]{0:T(128)S(1)} all-reduce(f32[4]{0:T(128)S(1)} %psum.33), channel_id=1, replica_groups=mesh['gy'=64,'gz'=4] {'gz'}, use_global_device_ids=true, to_apply=%region_10.11 | all-reduce | flops 4 | bytes 32 | tf_op jit(solution)/shard_map/psum | solution.py:23
  325.0 1.3 maximum_subtract_fusion.11
  327.7 3.4 collective-permute-start.15
  331.1 1.3 collective-permute-start.14
  332.9 8.4 %collective-permute-done.15 = f32[3,32,8,1]{3,2,1,0:T(8,128)S(1)} collective-permute-done((f32[3,32,8,1]{3,2,1,0:T(8,128)S(1)}, f32[3,32,8,1]{3,2,1,0:T(8,128)S(1)}, u32[]{:S(2)}, u32[]{:S(2)}) %collective-permute-start.15) | collective-permute-done | bytes 3104 | tf_op jit(solution)/shard_map/ppermute | solution.py:30
  (153 shorter events, 24.7 us)
Async XLA Ops:
  0.6 4.8 %copy-start = (bf16[3,32,8,256]{3,2,1,0:T(8,128)(2,1)S(1)}, bf16[3,32,8,256]{3,2,1,0:T(8,128)(2,1)}, u32[]{:S(2)}) copy-start(bf16[3,32,8,256]{3,2,1,0:T(8,128)(2,1)} %param.15) | copy-start | bytes 1179652
  1.7 12.9 %collective-permute-start.1 = (f32[3,32,8,1]{3,2,1,0:T(8,128)S(1)}, f32[3,32,8,1]{3,2,1,0:T(8,128)S(1)}, u32[]{:S(2)}, u32[]{:S(2)}) collective-permute-start(f32[3,32,8,1]{3,2,1,0:T(8,128)S(1)} %slice.413), channel_id=1, source_target_pairs={{1,0},{2,1},{3,2},{5,4},{6,5},{7,6},{9,8},{10,9},{11,10},{13,12},{... | collective-permute-start | bytes 9224 | tf_op jit(solution)/shard_map/ppermute | solution.py:30
  5.4 9.2 %collective-permute-start = (f32[3,1,8,256]{3,2,1,0:T(8,128)S(1)}, f32[3,1,8,256]{3,2,1,0:T(8,128)S(1)}, u32[]{:S(2)}, u32[]{:S(2)}) collective-permute-start(f32[3,1,8,256]{3,2,1,0:T(8,128)S(1)} %slice.410), channel_id=1, source_target_pairs={{4,0},{8,4},{12,8},{16,12},{20,16},{24,20},{28,24},{32,28},{36,32}... | collective-permute-start | bytes 73736 | tf_op jit(solution)/shard_map/ppermute | solution.py:30
  16.0 9.2 %copy-start.13 = (s32[32,8,256]{2,1,0:T(8,128)S(1)}, s32[32,8,256]{2,1,0:T(8,128)}, u32[]{:S(2)}) copy-start(s32[32,8,256]{2,1,0:T(8,128)} %param.26) | copy-start | bytes 786436
  16.0 9.2 %copy-start.30 = (s32[32,8,256]{2,1,0:T(8,128)S(1)}, s32[32,8,256]{2,1,0:T(8,128)}, u32[]{:S(2)}) copy-start(s32[32,8,256]{2,1,0:T(8,128)} %param.25) | copy-start | bytes 786436
  16.2 12.6 %collective-permute-start.3 = (f32[3,32,8,1]{3,2,1,0:T(8,128)S(1)}, f32[3,32,8,1]{3,2,1,0:T(8,128)S(1)}, u32[]{:S(2)}, u32[]{:S(2)}) collective-permute-start(f32[3,32,8,1]{3,2,1,0:T(8,128)S(1)} %slice.423), channel_id=1, source_target_pairs={{0,1},{1,2},{2,3},{4,5},{5,6},{6,7},{8,9},{9,10},{10,11},{12,13},{... | collective-permute-start | bytes 9224 | tf_op jit(solution)/shard_map/ppermute | solution.py:30
  19.8 9.0 %collective-permute-start.2 = (f32[3,1,8,256]{3,2,1,0:T(8,128)S(1)}, f32[3,1,8,256]{3,2,1,0:T(8,128)S(1)}, u32[]{:S(2)}, u32[]{:S(2)}) collective-permute-start(f32[3,1,8,256]{3,2,1,0:T(8,128)S(1)} %slice.420), channel_id=1, source_target_pairs={{0,4},{4,8},{8,12},{12,16},{16,20},{20,24},{24,28},{28,32},{32,36}... | collective-permute-start | bytes 73736 | tf_op jit(solution)/shard_map/ppermute | solution.py:30
  32.0 5.2 %copy-start.5 = (f32[2,32,8,256]{3,2,1,0:T(8,128)S(1)}, f32[2,32,8,256]{3,2,1,0:T(8,128)}, u32[]{:S(2)}) copy-start(f32[2,32,8,256]{3,2,1,0:T(8,128)} %param.24) | copy-start | bytes 1572868
  32.1 12.9 %collective-permute-start.5 = (f32[3,32,8,1]{3,2,1,0:T(8,128)S(1)}, f32[3,32,8,1]{3,2,1,0:T(8,128)S(1)}, u32[]{:S(2)}, u32[]{:S(2)}) collective-permute-start(f32[3,32,8,1]{3,2,1,0:T(8,128)S(1)} %slice.437), channel_id=1, source_target_pairs={{1,0},{2,1},{3,2},{5,4},{6,5},{7,6},{9,8},{10,9},{11,10},{13,12},{... | collective-permute-start | bytes 9224 | tf_op jit(solution)/shard_map/ppermute | solution.py:30
  35.9 9.1 %collective-permute-start.4 = (f32[3,1,8,256]{3,2,1,0:T(8,128)S(1)}, f32[3,1,8,256]{3,2,1,0:T(8,128)S(1)}, u32[]{:S(2)}, u32[]{:S(2)}) collective-permute-start(f32[3,1,8,256]{3,2,1,0:T(8,128)S(1)} %slice.434), channel_id=1, source_target_pairs={{4,0},{8,4},{12,8},{16,12},{20,16},{24,20},{28,24},{32,28},{36,32}... | collective-permute-start | bytes 73736 | tf_op jit(solution)/shard_map/ppermute | solution.py:30
  37.3 30.0 %copy-start.15 = (f32[1,32,8,256]{3,2,1,0:T(8,128)}, f32[1,32,8,256]{3,2,1,0:T(8,128)S(1)}, u32[]{:S(2)}) copy-start(f32[1,32,8,256]{3,2,1,0:T(8,128)S(1)} %get-tuple-element.91) | copy-start | bytes 786436
  37.3 30.0 %copy-start.17 = (f32[1,32,8,256]{3,2,1,0:T(8,128)}, f32[1,32,8,256]{3,2,1,0:T(8,128)S(1)}, u32[]{:S(2)}) copy-start(f32[1,32,8,256]{3,2,1,0:T(8,128)S(1)} %get-tuple-element.92) | copy-start | bytes 786436
  37.3 30.0 %copy-start.19 = (f32[1,32,8,256]{3,2,1,0:T(8,128)}, f32[1,32,8,256]{3,2,1,0:T(8,128)S(1)}, u32[]{:S(2)}) copy-start(f32[1,32,8,256]{3,2,1,0:T(8,128)S(1)} %get-tuple-element.93) | copy-start | bytes 786436
  37.3 30.0 %copy-start.21 = (f32[1,32,8,256]{3,2,1,0:T(8,128)}, f32[1,32,8,256]{3,2,1,0:T(8,128)S(1)}, u32[]{:S(2)}) copy-start(f32[1,32,8,256]{3,2,1,0:T(8,128)S(1)} %get-tuple-element.94) | copy-start | bytes 786436
  37.3 30.0 %copy-start.23 = (f32[1,32,8,256]{3,2,1,0:T(8,128)}, f32[1,32,8,256]{3,2,1,0:T(8,128)S(1)}, u32[]{:S(2)}) copy-start(f32[1,32,8,256]{3,2,1,0:T(8,128)S(1)} %get-tuple-element.95) | copy-start | bytes 786436
  45.8 13.6 %collective-permute-start.7 = (f32[3,32,8,1]{3,2,1,0:T(8,128)S(1)}, f32[3,32,8,1]{3,2,1,0:T(8,128)S(1)}, u32[]{:S(2)}, u32[]{:S(2)}) collective-permute-start(f32[3,32,8,1]{3,2,1,0:T(8,128)S(1)} %slice.447), channel_id=1, source_target_pairs={{0,1},{1,2},{2,3},{4,5},{5,6},{6,7},{8,9},{9,10},{10,11},{12,13},{... | collective-permute-start | bytes 9224 | tf_op jit(solution)/shard_map/ppermute | solution.py:30
  50.2 9.2 %collective-permute-start.6 = (f32[3,1,8,256]{3,2,1,0:T(8,128)S(1)}, f32[3,1,8,256]{3,2,1,0:T(8,128)S(1)}, u32[]{:S(2)}, u32[]{:S(2)}) collective-permute-start(f32[3,1,8,256]{3,2,1,0:T(8,128)S(1)} %slice.444), channel_id=1, source_target_pairs={{0,4},{4,8},{8,12},{12,16},{16,20},{20,24},{24,28},{28,32},{32,36}... | collective-permute-start | bytes 73736 | tf_op jit(solution)/shard_map/ppermute | solution.py:30
  64.0 14.0 %collective-permute-start.9 = (f32[3,32,8,1]{3,2,1,0:T(8,128)S(1)}, f32[3,32,8,1]{3,2,1,0:T(8,128)S(1)}, u32[]{:S(2)}, u32[]{:S(2)}) collective-permute-start(f32[3,32,8,1]{3,2,1,0:T(8,128)S(1)} %slice.461), channel_id=1, source_target_pairs={{1,0},{2,1},{3,2},{5,4},{6,5},{7,6},{9,8},{10,9},{11,10},{13,12},{... | collective-permute-start | bytes 9224 | tf_op jit(solution)/shard_map/ppermute | solution.py:30
  65.9 12.1 %collective-permute-start.8 = (f32[3,1,8,256]{3,2,1,0:T(8,128)S(1)}, f32[3,1,8,256]{3,2,1,0:T(8,128)S(1)}, u32[]{:S(2)}, u32[]{:S(2)}) collective-permute-start(f32[3,1,8,256]{3,2,1,0:T(8,128)S(1)} %slice.458), channel_id=1, source_target_pairs={{4,0},{8,4},{12,8},{16,12},{20,16},{24,20},{28,24},{32,28},{36,32}... | collective-permute-start | bytes 73736 | tf_op jit(solution)/shard_map/ppermute | solution.py:30
  78.5 14.2 %copy-start.9 = (f32[1,32,8,256]{3,2,1,0:T(8,128)}, f32[1,32,8,256]{3,2,1,0:T(8,128)S(1)}, u32[]{:S(2)}) copy-start(f32[1,32,8,256]{3,2,1,0:T(8,128)S(1)} %get-tuple-element.60) | copy-start | bytes 786436
  78.5 14.2 %copy-start.11 = (f32[1,32,8,256]{3,2,1,0:T(8,128)}, f32[1,32,8,256]{3,2,1,0:T(8,128)S(1)}, u32[]{:S(2)}) copy-start(f32[1,32,8,256]{3,2,1,0:T(8,128)S(1)} %get-tuple-element.61) | copy-start | bytes 786436
  80.0 12.7 %collective-permute-start.11 = (f32[3,32,8,1]{3,2,1,0:T(8,128)S(1)}, f32[3,32,8,1]{3,2,1,0:T(8,128)S(1)}, u32[]{:S(2)}, u32[]{:S(2)}) collective-permute-start(f32[3,32,8,1]{3,2,1,0:T(8,128)S(1)} %slice.471), channel_id=1, source_target_pairs={{0,1},{1,2},{2,3},{4,5},{5,6},{6,7},{8,9},{9,10},{10,11},{12,13},{... | collective-permute-start | bytes 9224 | tf_op jit(solution)/shard_map/ppermute | solution.py:30
  83.6 9.1 %collective-permute-start.10 = (f32[3,1,8,256]{3,2,1,0:T(8,128)S(1)}, f32[3,1,8,256]{3,2,1,0:T(8,128)S(1)}, u32[]{:S(2)}, u32[]{:S(2)}) collective-permute-start(f32[3,1,8,256]{3,2,1,0:T(8,128)S(1)} %slice.468), channel_id=1, source_target_pairs={{0,4},{4,8},{8,12},{12,16},{16,20},{20,24},{24,28},{28,32},{32,36}... | collective-permute-start | bytes 73736 | tf_op jit(solution)/shard_map/ppermute | solution.py:30
  307.1 4.4 %copy-start.16 = (f32[1,32,8,256]{3,2,1,0:T(8,128)S(1)}, f32[1,32,8,256]{3,2,1,0:T(8,128)}, u32[]{:S(2)}) copy-start(f32[1,32,8,256]{3,2,1,0:T(8,128)} %copy-done.15) | copy-start | bytes 786436
  307.1 4.4 %copy-start.18 = (f32[1,32,8,256]{3,2,1,0:T(8,128)S(1)}, f32[1,32,8,256]{3,2,1,0:T(8,128)}, u32[]{:S(2)}) copy-start(f32[1,32,8,256]{3,2,1,0:T(8,128)} %copy-done.17) | copy-start | bytes 786436
  307.1 4.4 %copy-start.20 = (f32[1,32,8,256]{3,2,1,0:T(8,128)S(1)}, f32[1,32,8,256]{3,2,1,0:T(8,128)}, u32[]{:S(2)}) copy-start(f32[1,32,8,256]{3,2,1,0:T(8,128)} %copy-done.19) | copy-start | bytes 786436
  307.1 4.4 %copy-start.22 = (f32[1,32,8,256]{3,2,1,0:T(8,128)S(1)}, f32[1,32,8,256]{3,2,1,0:T(8,128)}, u32[]{:S(2)}) copy-start(f32[1,32,8,256]{3,2,1,0:T(8,128)} %copy-done.21) | copy-start | bytes 786436
  308.3 16.7 %collective-permute-start.13 = (f32[3,32,8,1]{3,2,1,0:T(8,128)}, f32[3,32,8,1]{3,2,1,0:T(8,128)}, u32[]{:S(2)}, u32[]{:S(2)}) collective-permute-start(f32[3,32,8,1]{3,2,1,0:T(8,128)} %slice.483), channel_id=1, source_target_pairs={{1,0},{2,1},{3,2},{5,4},{6,5},{7,6},{9,8},{10,9},{11,10},{13,12},{... | collective-permute-start | bytes 9224 | tf_op jit(solution)/shard_map/ppermute | solution.py:30
  310.2 14.8 %collective-permute-start.12 = (f32[3,1,8,256]{3,2,1,0:T(8,128)S(1)}, f32[3,1,8,256]{3,2,1,0:T(8,128)S(1)}, u32[]{:S(2)}, u32[]{:S(2)}) collective-permute-start(f32[3,1,8,256]{3,2,1,0:T(8,128)S(1)} %slice.480), channel_id=1, source_target_pairs={{4,0},{8,4},{12,8},{16,12},{20,16},{24,20},{28,24},{32,28},{36,32}... | collective-permute-start | bytes 73736 | tf_op jit(solution)/shard_map/ppermute | solution.py:30
  327.5 13.8 %copy-start.1 = (f32[3,32,8,256]{3,2,1,0:T(8,128)}, f32[3,32,8,256]{3,2,1,0:T(8,128)S(1)}, u32[]{:S(2)}) copy-start(f32[3,32,8,256]{3,2,1,0:T(8,128)S(1)} %maximum_add_fusion.1) | copy-start | bytes 2359300
  327.7 13.6 %collective-permute-start.15 = (f32[3,32,8,1]{3,2,1,0:T(8,128)S(1)}, f32[3,32,8,1]{3,2,1,0:T(8,128)S(1)}, u32[]{:S(2)}, u32[]{:S(2)}) collective-permute-start(f32[3,32,8,1]{3,2,1,0:T(8,128)S(1)} %slice.493), channel_id=1, source_target_pairs={{0,1},{1,2},{2,3},{4,5},{5,6},{6,7},{8,9},{9,10},{10,11},{12,13},{... | collective-permute-start | bytes 9224 | tf_op jit(solution)/shard_map/ppermute | solution.py:30
  331.1 10.3 %collective-permute-start.14 = (f32[3,1,8,256]{3,2,1,0:T(8,128)S(1)}, f32[3,1,8,256]{3,2,1,0:T(8,128)S(1)}, u32[]{:S(2)}, u32[]{:S(2)}) collective-permute-start(f32[3,1,8,256]{3,2,1,0:T(8,128)S(1)} %slice.490), channel_id=1, source_target_pairs={{0,4},{4,8},{8,12},{12,16},{16,20},{20,24},{24,28},{28,32},{32,36}... | collective-permute-start | bytes 73736 | tf_op jit(solution)/shard_map/ppermute | solution.py:30
  (18 other events, 19.8 us)
